TPU v7x, 256 devices: a whole 4x4x8 slice. The times are simulated.
256 devices in a mesh: snap: 8 (over x, core), slab: 32 (over y, z).
Axes of the slice: x: 4, y: 4, z: 8, core: 2. Of those that a mesh axis runs over, the one named last changes fastest.
Arguments:
- velocity: bfloat16 [256, 3, 160, 8, 128], P('snap', None, 'slab'), may hold values from -10 to 10
Outputs:
- modes: bfloat16 [768, 32, 5120], P(None, 'slab', 'snap')
- factor: float32 [768, 768], replicated
All inputs are finite; a program needn't handle non-finite values.
Results may differ from a plain program's by a relative error of at most 0.0004.
The roundings to bfloat16 on the way count: a program that leaves them out, or rounds other values in their place, can miss the bound.
Values may be sent and summed in bfloat16 or wider, within the bound.
No kernel may reach another device: no remote copies, remote signals or barrier semaphores. Data moves between devices by JAX's collectives and lax.ppermute only.
A program may use at most 64 MiB of HBM per device.

v0:
```python
import jax
import jax.numpy as jnp
from jax import lax
from jax.sharding import PartitionSpec as P

stencil_weights = (4.0 / 5.0, -1.0 / 5.0, 4.0 / 105.0, -1.0 / 280.0)


def with_halo(block, sides, width):
    for axis, dim in sides:
        count = lax.axis_size(axis)
        forward = [(i, i + 1) for i in range(count - 1)]
        backward = [(target, source) for source, target in forward]
        low = lax.ppermute(
            lax.slice_in_dim(block, block.shape[dim] - width, None, axis=dim), axis, forward
        )
        high = lax.ppermute(lax.slice_in_dim(block, 0, width, axis=dim), axis, backward)
        block = jnp.concatenate([low, block, high], axis=dim)
    return block


def differ(padded, axis, length):
    total = None
    for offset in range(4):
        step = offset + 1
        ahead = lax.slice_in_dim(padded, 4 + step, 4 + step + length, axis=axis)
        behind = lax.slice_in_dim(padded, 4 - step, 4 - step + length, axis=axis)
        term = stencil_weights[offset] * (ahead - behind)
        total = term if total is None else total + term
    return total


def derive(field, axis):
    widths = [(0, 0)] * field.ndim
    widths[axis] = (4, 4)
    return differ(jnp.pad(field, widths), axis, field.shape[axis])


def reduce_entries(entries):
    share = lax.psum_scatter(entries, ("snap", "slab"), scatter_dimension=0, tiled=True)
    total = lax.all_gather(share, ("snap", "slab"), axis=0, tiled=True)
    return total


def padded_sum(entries):
    summed = reduce_entries(entries)
    return summed


def body(velocity):
    planes = velocity.shape[2]
    extended = with_halo(velocity, (("slab", 2),), 4)
    second_rim = extended[:, 1].astype(jnp.float32)
    third_rim = extended[:, 2].astype(jnp.float32)
    first = velocity[:, 0].astype(jnp.float32)
    second = velocity[:, 1].astype(jnp.float32)
    third = velocity[:, 2].astype(jnp.float32)
    omega_one = derive(third, 2) - derive(second, 3)
    omega_two = derive(first, 3) - differ(third_rim, 1, planes)
    omega_three = differ(second_rim, 1, planes) - derive(first, 2)
    vorticity = jnp.stack([omega_one, omega_two, omega_three], axis=1).astype(jnp.bfloat16)
    local_snaps = vorticity.shape[0]
    flat = vorticity.reshape(local_snaps, 3, -1)
    regrouped = lax.all_to_all(flat, "snap", split_axis=2, concat_axis=0, tiled=True)
    width = regrouped.shape[0] * 3
    matrix = regrouped.reshape(width, -1)
    rows = matrix.shape[1]
    gram = lax.dot_general(
        matrix, matrix, (((1,), (1,)), ((), ())), preferred_element_type=jnp.float32
    )
    total = padded_sum(gram.reshape(-1)).reshape(width, width)
    point_count = rows * lax.axis_size("snap") * lax.axis_size("slab")
    lower = jnp.linalg.cholesky(total / point_count)
    factor = lower.T
    solved = jax.scipy.linalg.solve_triangular(lower, matrix.astype(jnp.float32), lower=True)
    modes = solved.astype(jnp.bfloat16).reshape(width, 1, rows)
    return (modes, factor)


def solution(mesh):
    in_specs = (P("snap", None, "slab", None, None),)
    out_specs = (P(None, "slab", "snap"), P())
    return jax.shard_map(body, mesh=mesh, in_specs=in_specs, out_specs=out_specs, check_vma=False)
```

profile of v0, /device:TPU:1, one launch (start us, length us, event | category | flops | bytes accessed | tf_op | source)
XLA Modules:
  0.0 749.4 jit_solution(7124444804363547871)
XLA Ops:
  8.5 4.4 collective-permute-start
  13.9 15.1 %collective-permute-done = bf16[32,3,4,8,128]{4,3,2,1,0:T(8,128)(2,1)S(1)} collective-permute-done((bf16[32,3,4,8,128]{4,3,2,1,0:T(8,128)(2,1)S(1)}, bf16[32,3,4,8,128]{4,3,2,1,0:T(8,128)(2,1)S(1)}, u32[]{:S(2)}, u32[]{:S(2)}) %collective-permute-start) | collective-permute-done | bytes 786464 | tf_op jit(solution)/shard_map/ppermute | solution.py:14
  32.7 17.3 %collective-permute-done.1 = bf16[32,3,4,8,128]{4,3,2,0,1:T(8,128)(2,1)S(1)} collective-permute-done((bf16[32,3,4,8,128]{4,3,2,0,1:T(8,128)(2,1)S(1)}, bf16[32,3,4,8,128]{4,3,2,0,1:T(8,128)(2,1)S(1)}, u32[]{:S(2)}, u32[]{:S(2)}) %collective-permute-start.1) | collective-permute-done | bytes 786464 | tf_op jit(solution)/shard_map/ppermute | solution.py:17
  51.1 1.6 fusion.22
  52.8 2.3 fusion.29
  55.5 5.0 copy.42
  60.5 6.9 reshape.211
  67.5 20.5 %all_to_all.15 = bf16[8,2,30720]{2,1,0:T(2,128)(2,1)S(1)} all-to-all(bf16[8,2,30720]{2,1,0:T(2,128)(2,1)S(1)} %reshape.211), channel_id=1, replica_groups=mesh['snap'=8,'slab'=32] {'snap'}, dimensions={0} | all-to-all | bytes 1966080 | tf_op jit(solution)/shard_map/all_to_all | solution.py:64
  88.0 5.4 reshape.212
  93.4 5.4 copy.47
  101.6 1.6 reshape.180
  103.5 263.8 %all-reduce.8.cloned.1.call-done = f32[589824]{0:T(1024)} async-done(((f32[589824]{0:T(1024)}), f32[589824]{0:T(1024)}) %all-reduce.8.cloned.1.call-update) | async-done | bytes 2359312
  368.8 1.4 convert_element_type.53
  370.2 106.2 %all-gather.3.cloned.1.call-done = f32[256,1,2304]{2,1,0:T(1,128)} async-done(((f32[1,1,2304]{2,1,0:T(1,128)}), f32[256,1,2304]{2,1,0:T(1,128)}) %all-gather.3.cloned.1.call-update) | async-done | bytes 2359312 | tf_op jit(solution)/shard_map/all_gather | solution.py:41
  476.4 10.2 %multiply_reduce_fusion = f32[256,2304]{1,0:T(8,128)} fusion(f32[256,1,2304]{2,1,0:T(1,128)} %all-gather.3.cloned.1.call-done), kind=kLoop, calls=%fused_computation.20 | loop fusion | flops 589824 | bytes 4718592 | tf_op jit(solution)/shard_map/div | solution.py:73
  486.5 2.5 div.18
  489.0 2.3 copy.45
  491.4 2.0 fusion
  494.7 11.7 %cholesky.165 = f32[128,128]{1,0:T(8,128)S(1)} custom-call(f32[128,128]{1,0:T(8,128)S(1)} %cholesky.424), custom_call_target="Cholesky" | custom-call | tf_op jit(solution)/shard_map/jit(cholesky)/cholesky | solution.py:73
  506.5 9.8 %custom-call.47 = f32[1,128,128]{1,2,0:T(8,128)S(1)} custom-call(f32[1,128,128]{2,1,0:T(8,128)S(1)} %get-tuple-element.55), custom_call_target="InvertDiagBlocksLowerTriangular" | custom-call | tf_op jit(solution)/shard_map/jit(cholesky)/cholesky | solution.py:73
  517.9 1.4 convolution_subtract_fusion.2
  520.0 11.7 %cholesky.188 = f32[128,128]{1,0:T(8,128)S(1)} custom-call(f32[128,128]{1,0:T(8,128)S(1)} %cholesky.428), custom_call_target="Cholesky" | custom-call | tf_op jit(solution)/shard_map/jit(cholesky)/cholesky | solution.py:73
  531.7 9.9 %custom-call.48 = f32[1,128,128]{1,2,0:T(8,128)S(1)} custom-call(f32[1,128,128]{2,1,0:T(8,128)S(1)} %get-tuple-element.52), custom_call_target="InvertDiagBlocksLowerTriangular" | custom-call | tf_op jit(solution)/shard_map/jit(cholesky)/cholesky | solution.py:73
  543.0 1.5 convolution_subtract_fusion.5
  545.3 11.7 %cholesky.354 = f32[128,128]{1,0:T(8,128)S(1)} custom-call(f32[128,128]{1,0:T(8,128)S(1)} %cholesky.433), custom_call_target="Cholesky" | custom-call | tf_op jit(solution)/shard_map/jit(cholesky)/cholesky | solution.py:73
  557.7 9.8 %custom-call.49 = f32[1,128,128]{1,2,0:T(8,128)S(1)} custom-call(f32[1,128,128]{2,1,0:T(8,128)S(1)} %get-tuple-element.49), custom_call_target="InvertDiagBlocksLowerTriangular" | custom-call | tf_op jit(solution)/shard_map/jit(cholesky)/cholesky | solution.py:73
  568.8 1.6 convolution_subtract_fusion.6
  570.9 13.4 %cholesky.373 = f32[128,128]{1,0:T(8,128)} custom-call(f32[128,128]{1,0:T(8,128)} %cholesky.438), custom_call_target="Cholesky" | custom-call | tf_op jit(solution)/shard_map/jit(cholesky)/cholesky | solution.py:73
  584.3 1.5 select_reduce_fusion.2
  586.4 11.3 %custom-call.50 = f32[1,128,128]{1,2,0:T(8,128)} custom-call(f32[1,128,128]{2,1,0:T(8,128)} %get-tuple-element.46), custom_call_target="InvertDiagBlocksLowerTriangular" | custom-call | tf_op jit(solution)/shard_map/jit(cholesky)/cholesky | solution.py:73
  598.8 1.5 convolution_subtract_fusion.7
  600.3 12.3 %cholesky.392 = f32[128,128]{1,0:T(8,128)} custom-call(f32[128,128]{1,0:T(8,128)S(1)} %cholesky.443), custom_call_target="Cholesky" | custom-call | tf_op jit(solution)/shard_map/jit(cholesky)/cholesky | solution.py:73
  614.2 10.4 %custom-call.51 = f32[1,128,128]{1,2,0:T(8,128)} custom-call(f32[1,128,128]{2,1,0:T(8,128)S(1)} %get-tuple-element.43), custom_call_target="InvertDiagBlocksLowerTriangular" | custom-call | tf_op jit(solution)/shard_map/jit(cholesky)/cholesky | solution.py:73
  627.0 11.9 %cholesky.410 = f32[128,128]{1,0:T(8,128)S(1)} custom-call(f32[128,128]{1,0:T(8,128)S(1)} %convolution_subtract_fusion.8), custom_call_target="Cholesky" | custom-call | tf_op jit(solution)/shard_map/jit(cholesky)/cholesky | solution.py:73
  643.8 2.4 fusion.2
  646.3 3.2 copy.46
  649.5 20.4 %while.1 = (s32[]{:T(128)}, f32[768,768]{1,0:T(8,128)}, s32[6,2]{0,1:T(2,128)S(1)}, f32[6,128,128]{2,1,0:T(8,128)}, s32[]{:T(128)}) while((s32[]{:T(128)}, f32[768,768]{1,0:T(8,128)}, s32[6,2]{0,1:T(2,128)S(1)}, f32[6,128,128]{2,1,0:T(8,128)}, s32[]{:T(128)}) %tuple.50), condition=%wide.while_cond, body=%wide.while_body.sunk | while | flops 2 | bytes 132205 | solution.py:75
  650.1 2.8 bitcast_dynamic-update-slice_fusion.7
  653.5 2.8 bitcast_dynamic-update-slice_fusion.7
  656.9 2.8 bitcast_dynamic-update-slice_fusion.7
  660.3 2.8 bitcast_dynamic-update-slice_fusion.7
  663.7 2.8 bitcast_dynamic-update-slice_fusion.7
  667.1 2.7 bitcast_dynamic-update-slice_fusion.7
  669.9 59.8 %custom-call.52 = f32[6,128,128]{1,2,0:T(8,128)S(1)} custom-call(f32[6,128,128]{2,1,0:T(8,128)} %get-tuple-element.9), custom_call_target="InvertDiagBlocksLowerTriangular" | custom-call | tf_op jit(solution)/shard_map/jit(_solve_triangular)/triangular_solve | solution.py:75
  731.8 1.4 convolution_subtract_fusion
  733.7 1.8 convolution_subtract_fusion.4
  736.0 1.9 fusion.11
  738.5 2.2 convolution_subtract_fusion.3
  (87 shorter events, 35.8 us)
Async XLA Ops:
  7.2 22.0 %copy-start.2 = (bf16[32,3,5,8,128]{4,3,2,1,0:T(8,128)(2,1)S(1)}, bf16[32,3,5,8,128]{4,3,2,1,0:T(8,128)(2,1)}, u32[]{:S(2)}) copy-start(bf16[32,3,5,8,128]{4,3,2,1,0:T(8,128)(2,1)} %param.1) | copy-start | bytes 2949124
  7.2 360.1 %all-reduce.8.cloned.1.call-start = ((), (), s32[]{:S(2)}) async-start(), calls=%async_computation.2 | async-start | bytes 4718592
  8.5 20.6 %collective-permute-start = (bf16[32,3,4,8,128]{4,3,2,1,0:T(8,128)(2,1)S(1)}, bf16[32,3,4,8,128]{4,3,2,1,0:T(8,128)(2,1)S(1)}, u32[]{:S(2)}, u32[]{:S(2)}) collective-permute-start(bf16[32,3,4,8,128]{4,3,2,1,0:T(8,128)(2,1)S(1)} %slice.372), channel_id=1, source_target_pairs={{0,1},{1,2},{2,3},{3,4},{4,5},{5,6},{6,7},{7,8},{8,9},{9,10},{10,1... | collective-permute-start | bytes 2359304 | tf_op jit(solution)/shard_map/ppermute | solution.py:14
  29.5 1.6 copy-start.3
  29.5 20.5 %collective-permute-start.1 = (bf16[32,3,4,8,128]{4,3,2,0,1:T(8,128)(2,1)S(1)}, bf16[32,3,4,8,128]{4,3,2,0,1:T(8,128)(2,1)S(1)}, u32[]{:S(2)}, u32[]{:S(2)}) collective-permute-start(bf16[32,3,4,8,128]{4,3,2,0,1:T(8,128)(2,1)S(1)} %slice.429), channel_id=1, source_target_pairs={{1,0},{2,1},{3,2},{4,3},{5,4},{6,5},{7,6},{8,7},{9,8},{10,9},{11,1... | collective-permute-start | bytes 2359304 | tf_op jit(solution)/shard_map/ppermute | solution.py:17
  103.2 373.1 %all-gather.3.cloned.1.call-start = ((), (), s32[]{:S(2)}) async-start(), calls=%async_computation.1 | async-start | bytes 2368512 | tf_op jit(solution)/shard_map/all_gather | solution.py:41
  493.3 1.4 copy-start
  519.3 0.7 copy-start.4
  544.6 0.7 copy-start.5
  646.3 83.8 %copy-start.1 = (f32[768,640]{1,0:T(8,128)S(1)}, f32[768,640]{1,0:T(8,128)}, u32[]{:S(2)}) copy-start(f32[768,640]{1,0:T(8,128)} %convert_element_type.53) | copy-start | bytes 5898244
  741.2 0.9 copy-start.6
Sparse Core Ops, SparseCore 0:
  103.3 263.9 all-reduce.7
  371.4 104.8 all-gather.2
where the time goes:
time: 758 us; the launch traced here: 749 us
  waiting for transfers between devices  402 us (53%)
  other arithmetic  212 us (28%)
  local copies, waits for them, and re-layouts  63.8 us (8%)
  matrix products  25.8 us (3%)
  blocking collectives  20.5 us (3%)
  between operations  18.6 us (2%)
    unnamed x3, waiting for transfers between devices  264 us
    another operation x22, other arithmetic, body(): lower = jnp.linalg.cholesky(total / point_count)  130 us
    all_gather x1, waiting for transfers between devices, reduce_entries(): total = lax.all_gather(share, ('snap', 'slab'), axis=0, tiled=True)  106 us
    another operation x2, other arithmetic, body(): jax.scipy.linalg.solve_triangular(lower, matrix.astype(jnp.float32), lowe...  59.8 us
    unnamed x25, local copies, waits for them, and re-layouts  21.1 us
    all_to_all x1, blocking collectives, body(): lax.all_to_all(flat, 'snap', split_axis=2, concat_axis=0, tiled=True)  20.5 us
    another operation x18, local copies, waits for them, and re-layouts  20.4 us
    ppermute x1, waiting for transfers between devices, with_halo(): lax.ppermute(lax.slice_in_dim(block, 0, width, axis=dim), axis, backward)  17.3 us
  transfers between devices with their start and end apart: 4, of which 4 were waited for; matrix products, arithmetic and copies ran while one was open for 1% of the time, Pallas kernels for 0%

commit v1 on v0

--- a/solution.py
+++ b/solution.py
@@ -38,7 +38,8 @@
 
 def reduce_entries(entries):
     share = lax.psum_scatter(entries, ("snap", "slab"), scatter_dimension=0, tiled=True)
-    total = lax.all_gather(share, ("snap", "slab"), axis=0, tiled=True)
+    repeated = jnp.stack([share] * lax.axis_size(("snap", "slab")))
+    total = jnp.concatenate(lax.all_to_all(repeated, ("snap", "slab"), 0, 0), axis=0)
     return total
 
 

time: 758 us -> 724 us (0.955)
  waiting for transfers between devices: 402 us -> 355 us
  starting transfers between devices: 5.99 us -> 18.3 us
    all_gather x1 -> x0, waiting for transfers between devices: 106 us -> none  [reduce_entries(): total = lax.all_gather(share, ('snap', 'slab'), axis=0, tiled=True)]
    all_to_all x0 -> x1, waiting for transfers between devices: none -> 58.4 us  [reduce_entries(): lax.all_to_all(repeated, ('snap', 'slab'), 0, 0)]
    all_to_all x0 -> x1, starting transfers between devices: none -> 12.5 us  [reduce_entries(): lax.all_to_all(repeated, ('snap', 'slab'), 0, 0)]
    another operation x18 -> x19, local copies, waits for them, and re-layouts: 20.4 us -> 23 us
    unnamed x25 -> x24, local copies, waits for them, and re-layouts: 21.1 us -> 20.5 us
    unnamed x3 -> x2, waiting for transfers between devices: 264 us -> 264 us
where the time goes in v1:
time: 724 us; the launch traced here: 714 us
  waiting for transfers between devices  355 us (49%)
  other arithmetic  210 us (29%)
  local copies, waits for them, and re-layouts  65.8 us (9%)
  matrix products  25.8 us (4%)
  blocking collectives  20.5 us (3%)
  between operations  18.6 us (3%)
  starting transfers between devices  18.3 us (3%)
    unnamed x2, waiting for transfers between devices  264 us
    another operation x22, other arithmetic, body(): lower = jnp.linalg.cholesky(total / point_count)  130 us
    another operation x2, other arithmetic, body(): jax.scipy.linalg.solve_triangular(lower, matrix.astype(jnp.float32), lowe...  59.8 us
    all_to_all x1, waiting for transfers between devices, reduce_entries(): lax.all_to_all(repeated, ('snap', 'slab'), 0, 0)  58.4 us
    unnamed x24, local copies, waits for them, and re-layouts  20.5 us
    all_to_all x1, blocking collectives, body(): lax.all_to_all(flat, 'snap', split_axis=2, concat_axis=0, tiled=True)  20.5 us
    another operation x18, local copies, waits for them, and re-layouts  20.4 us
    ppermute x1, waiting for transfers between devices, with_halo(): lax.ppermute(lax.slice_in_dim(block, 0, width, axis=dim), axis, backward)  17.3 us
  transfers between devices with their start and end apart: 4, of which 4 were waited for; matrix products, arithmetic and copies ran while one was open for 1% of the time, Pallas kernels for 0%

profile of v1, /device:TPU:1, one launch (start us, length us, event | category | flops | bytes accessed | tf_op | source)
XLA Modules:
  0.0 714.2 jit_solution(7006768474954239122)
XLA Ops:
  8.5 4.4 collective-permute-start
  13.9 15.1 %collective-permute-done = bf16[32,3,4,8,128]{4,3,2,1,0:T(8,128)(2,1)S(1)} collective-permute-done((bf16[32,3,4,8,128]{4,3,2,1,0:T(8,128)(2,1)S(1)}, bf16[32,3,4,8,128]{4,3,2,1,0:T(8,128)(2,1)S(1)}, u32[]{:S(2)}, u32[]{:S(2)}) %collective-permute-start) | collective-permute-done | bytes 786464 | tf_op jit(solution)/shard_map/ppermute | solution.py:14
  32.7 17.3 %collective-permute-done.1 = bf16[32,3,4,8,128]{4,3,2,0,1:T(8,128)(2,1)S(1)} collective-permute-done((bf16[32,3,4,8,128]{4,3,2,0,1:T(8,128)(2,1)S(1)}, bf16[32,3,4,8,128]{4,3,2,0,1:T(8,128)(2,1)S(1)}, u32[]{:S(2)}, u32[]{:S(2)}) %collective-permute-start.1) | collective-permute-done | bytes 786464 | tf_op jit(solution)/shard_map/ppermute | solution.py:17
  51.1 1.6 fusion.22
  52.8 2.3 fusion.29
  55.5 5.0 copy.42
  60.5 6.9 reshape.213
  67.5 20.5 %all_to_all.21 = bf16[8,2,30720]{2,1,0:T(2,128)(2,1)S(1)} all-to-all(bf16[8,2,30720]{2,1,0:T(2,128)(2,1)S(1)} %reshape.213), channel_id=1, replica_groups=mesh['snap'=8,'slab'=32] {'snap'}, dimensions={0} | all-to-all | bytes 1966080 | tf_op jit(solution)/shard_map/all_to_all | solution.py:65
  88.0 5.4 reshape.214
  93.4 5.4 copy.47
  101.6 1.6 reshape.187
  103.2 264.1 %all-reduce.8.cloned.1.call-done = f32[589824]{0:T(1024)} async-done(((f32[589824]{0:T(1024)}), f32[589824]{0:T(1024)}) %all-reduce.8.cloned.1.call-update) | async-done | bytes 2359312
  368.1 2.6 stack.14
  370.7 12.5 %all-to-all-start.1 = ((f32[256,1,2304]{2,1,0:T(1,128)}), f32[256,1,2304]{2,1,0:T(1,128)S(1)}, u32[]{:S(2)}, u32[]{:S(2)}) async-start(f32[256,1,2304]{2,1,0:T(1,128)} %stack.14), calls=%async_computation.1 | async-start | bytes 4718592 | tf_op jit(solution)/shard_map/all_to_all | solution.py:42
  383.3 1.4 convert_element_type.53
  384.7 58.4 %all-to-all-done.1 = f32[256,1,2304]{2,1,0:T(1,128)S(1)} async-done(((f32[256,1,2304]{2,1,0:T(1,128)}), f32[256,1,2304]{2,1,0:T(1,128)S(1)}, u32[]{:S(2)}, u32[]{:S(2)}) %all-to-all-start.1) | async-done | bytes 2359328 | tf_op jit(solution)/shard_map/all_to_all | solution.py:42
  443.1 8.2 %multiply_reduce_fusion = f32[256,2304]{1,0:T(8,128)} fusion(f32[256,1,2304]{2,1,0:T(1,128)S(1)} %all-to-all-done.1), kind=kLoop, calls=%fused_computation.21 | loop fusion | flops 589824 | bytes 4718592 | tf_op jit(solution)/shard_map/div | solution.py:74
  451.3 2.5 div.18
  453.8 2.3 copy.45
  456.1 2.0 fusion
  459.5 11.7 %cholesky.165 = f32[128,128]{1,0:T(8,128)S(1)} custom-call(f32[128,128]{1,0:T(8,128)S(1)} %cholesky.424), custom_call_target="Cholesky" | custom-call | tf_op jit(solution)/shard_map/jit(cholesky)/cholesky | solution.py:74
  471.2 9.8 %custom-call.47 = f32[1,128,128]{1,2,0:T(8,128)S(1)} custom-call(f32[1,128,128]{2,1,0:T(8,128)S(1)} %get-tuple-element.55), custom_call_target="InvertDiagBlocksLowerTriangular" | custom-call | tf_op jit(solution)/shard_map/jit(cholesky)/cholesky | solution.py:74
  484.8 11.7 %cholesky.188 = f32[128,128]{1,0:T(8,128)S(1)} custom-call(f32[128,128]{1,0:T(8,128)S(1)} %cholesky.428), custom_call_target="Cholesky" | custom-call | tf_op jit(solution)/shard_map/jit(cholesky)/cholesky | solution.py:74
  496.5 9.9 %custom-call.48 = f32[1,128,128]{1,2,0:T(8,128)S(1)} custom-call(f32[1,128,128]{2,1,0:T(8,128)S(1)} %get-tuple-element.52), custom_call_target="InvertDiagBlocksLowerTriangular" | custom-call | tf_op jit(solution)/shard_map/jit(cholesky)/cholesky | solution.py:74
  507.8 1.5 convolution_subtract_fusion.5
  510.0 11.7 %cholesky.354 = f32[128,128]{1,0:T(8,128)S(1)} custom-call(f32[128,128]{1,0:T(8,128)S(1)} %cholesky.433), custom_call_target="Cholesky" | custom-call | tf_op jit(solution)/shard_map/jit(cholesky)/cholesky | solution.py:74
  522.5 9.8 %custom-call.49 = f32[1,128,128]{1,2,0:T(8,128)S(1)} custom-call(f32[1,128,128]{2,1,0:T(8,128)S(1)} %get-tuple-element.49), custom_call_target="InvertDiagBlocksLowerTriangular" | custom-call | tf_op jit(solution)/shard_map/jit(cholesky)/cholesky | solution.py:74
  533.5 1.6 convolution_subtract_fusion.6
  535.7 13.4 %cholesky.373 = f32[128,128]{1,0:T(8,128)} custom-call(f32[128,128]{1,0:T(8,128)} %cholesky.438), custom_call_target="Cholesky" | custom-call | tf_op jit(solution)/shard_map/jit(cholesky)/cholesky | solution.py:74
  549.1 1.5 select_reduce_fusion.2
  551.2 11.3 %custom-call.50 = f32[1,128,128]{1,2,0:T(8,128)} custom-call(f32[1,128,128]{2,1,0:T(8,128)} %get-tuple-element.46), custom_call_target="InvertDiagBlocksLowerTriangular" | custom-call | tf_op jit(solution)/shard_map/jit(cholesky)/cholesky | solution.py:74
  563.5 1.5 convolution_subtract_fusion.7
  565.0 12.3 %cholesky.392 = f32[128,128]{1,0:T(8,128)} custom-call(f32[128,128]{1,0:T(8,128)S(1)} %cholesky.443), custom_call_target="Cholesky" | custom-call | tf_op jit(solution)/shard_map/jit(cholesky)/cholesky | solution.py:74
  578.9 10.4 %custom-call.51 = f32[1,128,128]{1,2,0:T(8,128)} custom-call(f32[1,128,128]{2,1,0:T(8,128)S(1)} %get-tuple-element.43), custom_call_target="InvertDiagBlocksLowerTriangular" | custom-call | tf_op jit(solution)/shard_map/jit(cholesky)/cholesky | solution.py:74
  591.7 11.9 %cholesky.410 = f32[128,128]{1,0:T(8,128)S(1)} custom-call(f32[128,128]{1,0:T(8,128)S(1)} %convolution_subtract_fusion.8), custom_call_target="Cholesky" | custom-call | tf_op jit(solution)/shard_map/jit(cholesky)/cholesky | solution.py:74
  608.6 2.4 fusion.2
  611.0 3.2 copy.46
  614.2 20.4 %while.1 = (s32[]{:T(128)}, f32[768,768]{1,0:T(8,128)}, s32[6,2]{0,1:T(2,128)S(1)}, f32[6,128,128]{2,1,0:T(8,128)}, s32[]{:T(128)}) while((s32[]{:T(128)}, f32[768,768]{1,0:T(8,128)}, s32[6,2]{0,1:T(2,128)S(1)}, f32[6,128,128]{2,1,0:T(8,128)}, s32[]{:T(128)}) %tuple.50), condition=%wide.while_cond, body=%wide.while_body.sunk | while | flops 2 | bytes 132205 | solution.py:76
  614.8 2.8 bitcast_dynamic-update-slice_fusion.7
  618.2 2.8 bitcast_dynamic-update-slice_fusion.7
  621.6 2.8 bitcast_dynamic-update-slice_fusion.7
  625.1 2.8 bitcast_dynamic-update-slice_fusion.7
  628.5 2.8 bitcast_dynamic-update-slice_fusion.7
  631.9 2.7 bitcast_dynamic-update-slice_fusion.7
  634.6 59.8 %custom-call.52 = f32[6,128,128]{1,2,0:T(8,128)S(1)} custom-call(f32[6,128,128]{2,1,0:T(8,128)} %get-tuple-element.9), custom_call_target="InvertDiagBlocksLowerTriangular" | custom-call | tf_op jit(solution)/shard_map/jit(_solve_triangular)/triangular_solve | solution.py:76
  698.5 1.8 convolution_subtract_fusion.4
  700.8 1.9 fusion.11
  703.3 2.2 convolution_subtract_fusion.3
  (86 shorter events, 37.8 us)
Async XLA Ops:
  7.2 22.0 %copy-start.2 = (bf16[32,3,5,8,128]{4,3,2,1,0:T(8,128)(2,1)S(1)}, bf16[32,3,5,8,128]{4,3,2,1,0:T(8,128)(2,1)}, u32[]{:S(2)}) copy-start(bf16[32,3,5,8,128]{4,3,2,1,0:T(8,128)(2,1)} %param.1) | copy-start | bytes 2949124
  7.2 360.1 %all-reduce.8.cloned.1.call-start = ((), (), s32[]{:S(2)}) async-start(), calls=%async_computation.2 | async-start | bytes 4718592
  8.5 20.6 %collective-permute-start = (bf16[32,3,4,8,128]{4,3,2,1,0:T(8,128)(2,1)S(1)}, bf16[32,3,4,8,128]{4,3,2,1,0:T(8,128)(2,1)S(1)}, u32[]{:S(2)}, u32[]{:S(2)}) collective-permute-start(bf16[32,3,4,8,128]{4,3,2,1,0:T(8,128)(2,1)S(1)} %slice.372), channel_id=1, source_target_pairs={{0,1},{1,2},{2,3},{3,4},{4,5},{5,6},{6,7},{7,8},{8,9},{9,10},{10,1... | collective-permute-start | bytes 2359304 | tf_op jit(solution)/shard_map/ppermute | solution.py:14
  29.5 1.6 copy-start.3
  29.5 20.5 %collective-permute-start.1 = (bf16[32,3,4,8,128]{4,3,2,0,1:T(8,128)(2,1)S(1)}, bf16[32,3,4,8,128]{4,3,2,0,1:T(8,128)(2,1)S(1)}, u32[]{:S(2)}, u32[]{:S(2)}) collective-permute-start(bf16[32,3,4,8,128]{4,3,2,0,1:T(8,128)(2,1)S(1)} %slice.429), channel_id=1, source_target_pairs={{1,0},{2,1},{3,2},{4,3},{5,4},{6,5},{7,6},{8,7},{9,8},{10,9},{11,1... | collective-permute-start | bytes 2359304 | tf_op jit(solution)/shard_map/ppermute | solution.py:17
  370.7 72.4 %all-to-all-start.1 = ((f32[256,1,2304]{2,1,0:T(1,128)}), f32[256,1,2304]{2,1,0:T(1,128)S(1)}, u32[]{:S(2)}, u32[]{:S(2)}) async-start(f32[256,1,2304]{2,1,0:T(1,128)} %stack.14), calls=%async_computation.1 | async-start | bytes 4718592 | tf_op jit(solution)/shard_map/all_to_all | solution.py:42
  458.1 1.4 copy-start
  484.0 0.7 copy-start.4
  509.3 0.7 copy-start.5
  611.0 83.8 %copy-start.1 = (f32[768,640]{1,0:T(8,128)S(1)}, f32[768,640]{1,0:T(8,128)}, u32[]{:S(2)}) copy-start(f32[768,640]{1,0:T(8,128)} %convert_element_type.53) | copy-start | bytes 5898244
  706.0 0.9 copy-start.6
Sparse Core Ops, SparseCore 0:
  103.3 263.9 all-reduce.7
